TPU v7x, 32 devices: a whole 2x2x4 slice. The times are simulated.
32 devices in a mesh: mem: 4 (over y, core), lat: 4 (over z), lon: 2 (over x).
Axes of the slice: x: 2, y: 2, z: 4, core: 2. Of those that a mesh axis runs over, the one named last changes fastest.
Arguments:
- perturbations: bfloat16 [4, 8, 128, 256], P('mem', None, 'lat', 'lon'), may hold values from -6 to 6
- control: float32 [4, 8, 128, 256], P('mem', None, 'lat', 'lon'), may hold values from -6 to 6
- diffusivity: float32 [8, 128, 256], P(None, 'lat', 'lon'), may hold values from 0.03 to 0.24
- obs_cells: int32 [32, 512], P(('mem', 'lat', 'lon')), may hold values from 0 to 8191
- obs_counts: int32 [32], P(('mem', 'lat', 'lon')), may hold values from 256 to 512, as said below
- innovations: float32 [32, 512], P(('mem', 'lat', 'lon')), may hold values from -8 to 8
- obs_precision: float32 [32, 512], P(('mem', 'lat', 'lon')), may hold values from 0.5 to 2
Outputs:
- analysis_control: float32 [4, 8, 128, 256], P('mem', None, 'lat', 'lon')
Inputs may be any that keep to these rules, and one draw needn't show every extreme that they name: `obs_cells`: an entry names a cell of its own tile, counted as level times 8 * 128 plus tile row times 128 plus tile column; one cell may be named by several slots. `obs_counts`: slots at and beyond a tile's count are ignored; in every draw some tile is full.
All inputs are finite; a program needn't handle non-finite values.
Results may differ from a plain program's by a relative error of at most 0.0003.
Values sent between devices are 32-bit elements; how exact they have to be, the bound alone decides.
A program may use at most 64 MiB of HBM per device.

v0:
```python
import math

import jax
import jax.numpy as jnp
from jax import lax
from jax.sharding import PartitionSpec as P

SWEEPS = 4
STEPS = 2


huber_edge = 1.5
step_length = 0.5


def with_halo(cells, sides, width):
    for axis, dim in sides:
        count = lax.axis_size(axis)
        head = lax.slice_in_dim(cells, 0, width, axis=dim)
        tail = lax.slice_in_dim(cells, cells.shape[dim] - width, cells.shape[dim], axis=dim)
        cells = jnp.concatenate(
            [
                lax.ppermute(tail, axis, [(i, (i + 1) % count) for i in range(count)]),
                cells,
                lax.ppermute(head, axis, [((i + 1) % count, i) for i in range(count)]),
            ],
            axis=dim,
        )
    return cells


def inside_rows(lat_rows, margin):
    first_row = lax.axis_index("lat") * lat_rows - margin
    global_rows = first_row + jnp.arange(lat_rows + 2 * margin, dtype=jnp.int32)
    total_rows = lat_rows * lax.axis_size("lat")
    return ((global_rows >= 0) & (global_rows < total_rows)).astype(jnp.float32)[None, :, None]


def stencil(padded):
    center = padded[:, 1:-1, 1:-1]
    laplace_term = (
        padded[:, :-2, 1:-1]
        + padded[:, 2:, 1:-1]
        + padded[:, 1:-1, :-2]
        + padded[:, 1:-1, 2:]
        - 4.0 * center
    )
    return (laplace_term, center)


def smooth_deep(state_field, kappa_rim):
    lat_rows = state_field.shape[1]
    padded = with_halo(state_field, (("lat", 1), ("lon", 2)), SWEEPS)
    padded = padded * inside_rows(lat_rows, SWEEPS)
    for sweep_index in range(SWEEPS):
        offset = sweep_index + 1
        local_kappa = kappa_rim[
            :, offset : kappa_rim.shape[1] - offset, offset : kappa_rim.shape[2] - offset
        ]
        laplace_term, center = stencil(padded)
        padded = (center + local_kappa * laplace_term) * inside_rows(lat_rows, SWEEPS - offset)
    return padded


def adjoint_deep(state_field, kappa_rim):
    lat_rows = state_field.shape[1]
    padded = with_halo(state_field, (("lat", 1), ("lon", 2)), SWEEPS)
    padded = padded * inside_rows(lat_rows, SWEEPS)
    for sweep_index in range(SWEEPS):
        local_kappa = kappa_rim[
            :,
            sweep_index : kappa_rim.shape[1] - sweep_index,
            sweep_index : kappa_rim.shape[2] - sweep_index,
        ]
        laplace_term, center = stencil(local_kappa * padded)
        padded = (padded[:, 1:-1, 1:-1] + laplace_term) * inside_rows(
            lat_rows, SWEEPS - sweep_index - 1
        )
    return padded


def per_device(
    perturbations, control, diffusivity, obs_cells, obs_counts, innovations, obs_precision
):
    members = lax.axis_size("mem")
    weight = 1.0 / math.sqrt(members - 1)
    member_x = perturbations[0]
    alpha_now = control[0]
    live_slots = (
        jnp.arange(obs_cells.shape[1], dtype=jnp.int32)[None, :] < obs_counts[:, None]
    ).astype(jnp.float32)
    masked_weight = obs_precision * live_slots
    kappa_rim = with_halo(diffusivity, (("lat", 1), ("lon", 2)), SWEEPS)
    for step_index in range(STEPS):
        smoothed = smooth_deep(alpha_now, kappa_rim)
        member_term = member_x.astype(jnp.float32) * smoothed
        owned_piece = lax.psum_scatter(member_term, "mem", scatter_dimension=1, tiled=True)
        increment = weight * owned_piece
        tile_cells = obs_cells[0]
        observed = increment.reshape(-1)[tile_cells]
        misfit = (observed - innovations[0]) * masked_weight[0]
        pulled = jnp.clip(misfit, -huber_edge, huber_edge) * masked_weight[0]
        tile_field = (
            jnp.zeros((increment.size,), jnp.float32)
            .at[tile_cells]
            .add(pulled)
            .reshape(increment.shape)
        )
        forcing = lax.all_gather(tile_field, "mem", axis=1, tiled=True)
        source = weight * member_x.astype(jnp.float32) * forcing
        gradient = alpha_now + adjoint_deep(source, kappa_rim)
        alpha_now = alpha_now - step_length * gradient
    return alpha_now[None]


def solution(mesh):
    return jax.shard_map(
        per_device,
        mesh=mesh,
        in_specs=(
            P("mem", None, "lat", "lon"),
            P("mem", None, "lat", "lon"),
            P(None, "lat", "lon"),
            P(("mem", "lat", "lon"), None),
            P(("mem", "lat", "lon")),
            P(("mem", "lat", "lon"), None),
            P(("mem", "lat", "lon"), None),
        ),
        out_specs=P("mem", None, "lat", "lon"),
        check_vma=False,
    )
```

profile of v0, /device:TPU:0, one launch (start us, length us, event | category | flops | bytes accessed | tf_op | source)
XLA Modules:
  0.0 161.3 jit_solution(4320232397216367744)
XLA Ops:
  7.4 3.1 %collective-permute-start = (f32[8,4,128]{2,1,0:T(4,128)S(1)}, f32[8,4,128]{2,1,0:T(4,128)S(1)}, u32[]{:S(2)}, u32[]{:S(2)}) collective-permute-start(f32[8,4,128]{2,1,0:T(4,128)S(1)} %get-tuple-element.37), channel_id=1, source_target_pairs={{0,2},{2,4},{4,6},{6,0},{1,3},{3,5},{5,7},{7,1},{8,10},{10,12},{12... | collective-permute-start | bytes 49160 | tf_op jit(solution)/shard_map/ppermute | solution.py:23
  10.4 2.1 %collective-permute-start.1 = (f32[8,4,128]{2,1,0:T(4,128)S(1)}, f32[8,4,128]{2,1,0:T(4,128)S(1)}, u32[]{:S(2)}, u32[]{:S(2)}) collective-permute-start(f32[8,4,128]{2,1,0:T(4,128)S(1)} %get-tuple-element.38), channel_id=1, source_target_pairs={{2,0},{4,2},{6,4},{0,6},{3,1},{5,3},{7,5},{1,7},{10,8},{12,10},{14... | collective-permute-start | bytes 49160 | tf_op jit(solution)/shard_map/ppermute | solution.py:25
  13.3 3.8 %collective-permute-start.5 = (f32[8,4,128]{2,1,0:T(4,128)S(1)}, f32[8,4,128]{2,1,0:T(4,128)S(1)}, u32[]{:S(2)}, u32[]{:S(2)}) collective-permute-start(f32[8,4,128]{2,1,0:T(4,128)S(1)} %get-tuple-element.40), channel_id=1, source_target_pairs={{2,0},{4,2},{6,4},{0,6},{3,1},{5,3},{7,5},{1,7},{10,8},{12,10},{14... | collective-permute-start | bytes 49160 | tf_op jit(solution)/shard_map/ppermute | solution.py:25
  23.3 2.8 %collective-permute-done.6 = f32[8,40,4]{2,1,0:T(8,128)S(1)} collective-permute-done((f32[8,40,4]{2,1,0:T(8,128)S(1)}, f32[8,40,4]{2,1,0:T(8,128)S(1)}, u32[]{:S(2)}, u32[]{:S(2)}) %collective-permute-start.6) | collective-permute-done | bytes 5152 | tf_op jit(solution)/shard_map/ppermute | solution.py:23
  26.1 3.5 %collective-permute-done.7 = f32[8,40,4]{2,1,0:T(8,128)S(1)} collective-permute-done((f32[8,40,4]{2,1,0:T(8,128)S(1)}, f32[8,40,4]{2,1,0:T(8,128)S(1)}, u32[]{:S(2)}, u32[]{:S(2)}) %collective-permute-start.7) | collective-permute-done | bytes 5152 | tf_op jit(solution)/shard_map/ppermute | solution.py:25
  29.8 2.5 %collective-permute-done.2 = f32[8,40,4]{2,1,0:T(8,128)S(1)} collective-permute-done((f32[8,40,4]{2,1,0:T(8,128)S(1)}, f32[8,40,4]{2,1,0:T(8,128)S(1)}, u32[]{:S(2)}, u32[]{:S(2)}) %collective-permute-start.2) | collective-permute-done | bytes 5152 | tf_op jit(solution)/shard_map/ppermute | solution.py:23
  32.3 1.8 %collective-permute-done.3 = f32[8,40,4]{2,1,0:T(8,128)S(1)} collective-permute-done((f32[8,40,4]{2,1,0:T(8,128)S(1)}, f32[8,40,4]{2,1,0:T(8,128)S(1)}, u32[]{:S(2)}, u32[]{:S(2)}) %collective-permute-start.3) | collective-permute-done | bytes 5152 | tf_op jit(solution)/shard_map/ppermute | solution.py:25
  37.8 20.2 %reduce-scatter.3.cloned.1.call-done = f32[8,8,128]{2,1,0:T(8,128)} async-done(((f32[8,32,128]{2,1,0:T(8,128)}), f32[8,8,128]{2,1,0:T(8,128)}) %reduce-scatter.3.cloned.1.call-update) | async-done | bytes 32784 | tf_op jit(solution)/shard_map/reduce_scatter | solution.py:97
  58.8 3.1 %gather_fusion = f32[512]{0:T(512)S(1)} fusion(f32[8192]{0:T(1024)S(1)} %multiply_bitcast_fusion.1, s32[1024]{0:T(1024)S(1)} %pad_clamp_fusion), kind=kCustom, calls=%fused_computation | custom fusion | bytes 6144 | tf_op jit(solution)/shard_map/gather | solution.py:100
  62.7 3.3 %scatter_custom_fusion = f32[8192]{0:T(1024)S(1)} fusion(s32[512]{0:T(512)S(1)} %bitcast.31, f32[512]{0:T(512)S(1)} %clamp_multiply_fusion.1, f32[]{:T(128)} %constant.17.clone.1), kind=kCustom, calls=%fused_computation.148 | custom fusion | flops 512 | bytes 32772 | tf_op jit(solution)/shard_map/scatter-add | solution.py:106
  65.9 5.4 %all_gather.6 = f32[8,32,128]{2,1,0:T(8,128)S(1)} all-gather(f32[8,8,128]{2,1,0:T(8,128)S(1)} %bitcast.27), channel_id=1, replica_groups=mesh['mem'=4,'lat'=4,'lon'=2] {'mem'}, dimensions={1}, use_global_device_ids=true | all-gather | bytes 163840 | tf_op jit(solution)/shard_map/all_gather | solution.py:109
  72.9 2.3 %collective-permute-start.9 = (f32[8,4,128]{2,1,0:T(4,128)S(1)}, f32[8,4,128]{2,1,0:T(4,128)S(1)}, u32[]{:S(2)}, u32[]{:S(2)}) collective-permute-start(f32[8,4,128]{2,1,0:T(4,128)S(1)} %get-tuple-element.36), channel_id=1, source_target_pairs={{2,0},{4,2},{6,4},{0,6},{3,1},{5,3},{7,5},{1,7},{10,8},{12,10},{14... | collective-permute-start | bytes 49160 | tf_op jit(solution)/shard_map/ppermute | solution.py:25
  79.2 5.0 %collective-permute-done.10 = f32[8,40,4]{2,1,0:T(8,128)S(1)} collective-permute-done((f32[8,40,4]{2,1,0:T(8,128)S(1)}, f32[8,40,4]{2,1,0:T(8,128)S(1)}, u32[]{:S(2)}, u32[]{:S(2)}) %collective-permute-start.10) | collective-permute-done | bytes 5152 | tf_op jit(solution)/shard_map/ppermute | solution.py:23
  84.2 1.8 %collective-permute-done.11 = f32[8,40,4]{2,1,0:T(8,128)S(1)} collective-permute-done((f32[8,40,4]{2,1,0:T(8,128)S(1)}, f32[8,40,4]{2,1,0:T(8,128)S(1)}, u32[]{:S(2)}, u32[]{:S(2)}) %collective-permute-start.11) | collective-permute-done | bytes 5152 | tf_op jit(solution)/shard_map/ppermute | solution.py:25
  89.2 2.9 %collective-permute-start.13 = (f32[8,4,128]{2,1,0:T(4,128)S(1)}, f32[8,4,128]{2,1,0:T(4,128)S(1)}, u32[]{:S(2)}, u32[]{:S(2)}) collective-permute-start(f32[8,4,128]{2,1,0:T(4,128)S(1)} %get-tuple-element.34), channel_id=1, source_target_pairs={{2,0},{4,2},{6,4},{0,6},{3,1},{5,3},{7,5},{1,7},{10,8},{12,10},{14... | collective-permute-start | bytes 49160 | tf_op jit(solution)/shard_map/ppermute | solution.py:25
  96.1 3.3 %collective-permute-done.14 = f32[8,40,4]{2,1,0:T(8,128)S(1)} collective-permute-done((f32[8,40,4]{2,1,0:T(8,128)S(1)}, f32[8,40,4]{2,1,0:T(8,128)S(1)}, u32[]{:S(2)}, u32[]{:S(2)}) %collective-permute-start.14) | collective-permute-done | bytes 5152 | tf_op jit(solution)/shard_map/ppermute | solution.py:23
  99.4 1.8 %collective-permute-done.15 = f32[8,40,4]{2,1,0:T(8,128)S(1)} collective-permute-done((f32[8,40,4]{2,1,0:T(8,128)S(1)}, f32[8,40,4]{2,1,0:T(8,128)S(1)}, u32[]{:S(2)}, u32[]{:S(2)}) %collective-permute-start.15) | collective-permute-done | bytes 5152 | tf_op jit(solution)/shard_map/ppermute | solution.py:25
  103.8 20.3 %reduce-scatter.5.cloned.1.call-done = f32[8,8,128]{2,1,0:T(8,128)} async-done(((f32[8,32,128]{2,1,0:T(8,128)}), f32[8,8,128]{2,1,0:T(8,128)}) %reduce-scatter.5.cloned.1.call-update) | async-done | bytes 32784 | tf_op jit(solution)/shard_map/reduce_scatter | solution.py:97
  124.8 3.1 %gather_fusion.1 = f32[512]{0:T(512)S(1)} fusion(f32[8192]{0:T(1024)S(1)} %multiply_bitcast_fusion, s32[1024]{0:T(1024)S(1)} %pad_clamp_fusion), kind=kCustom, calls=%fused_computation.1 | custom fusion | bytes 6144 | tf_op jit(solution)/shard_map/gather | solution.py:100
  128.0 3.3 %scatter_custom_fusion.1 = f32[8192]{0:T(1024)S(1)} fusion(s32[512]{0:T(512)S(1)} %bitcast.32, f32[512]{0:T(512)S(1)} %clamp_multiply_fusion, f32[]{:T(128)} %constant.17.clone.1), kind=kCustom, calls=%fused_computation.146 | custom fusion | flops 512 | bytes 32772 | tf_op jit(solution)/shard_map/scatter-add | solution.py:106
  131.3 5.6 %all_gather.7 = f32[8,32,128]{2,1,0:T(8,128)S(1)} all-gather(f32[8,8,128]{2,1,0:T(8,128)S(1)} %bitcast.26), channel_id=1, replica_groups=mesh['mem'=4,'lat'=4,'lon'=2] {'mem'}, dimensions={1}, use_global_device_ids=true | all-gather | bytes 163840 | tf_op jit(solution)/shard_map/all_gather | solution.py:109
  138.4 2.3 %collective-permute-start.17 = (f32[8,4,128]{2,1,0:T(4,128)S(1)}, f32[8,4,128]{2,1,0:T(4,128)S(1)}, u32[]{:S(2)}, u32[]{:S(2)}) collective-permute-start(f32[8,4,128]{2,1,0:T(4,128)S(1)} %get-tuple-element.32), channel_id=1, source_target_pairs={{2,0},{4,2},{6,4},{0,6},{3,1},{5,3},{7,5},{1,7},{10,8},{12,10},{14... | collective-permute-start | bytes 49160 | tf_op jit(solution)/shard_map/ppermute | solution.py:25
  144.7 5.0 %collective-permute-done.18 = f32[8,40,4]{2,1,0:T(8,128)S(1)} collective-permute-done((f32[8,40,4]{2,1,0:T(8,128)S(1)}, f32[8,40,4]{2,1,0:T(8,128)S(1)}, u32[]{:S(2)}, u32[]{:S(2)}) %collective-permute-start.18) | collective-permute-done | bytes 5152 | tf_op jit(solution)/shard_map/ppermute | solution.py:23
  149.8 1.8 %collective-permute-done.19 = f32[8,40,4]{2,1,0:T(8,128)S(1)} collective-permute-done((f32[8,40,4]{2,1,0:T(8,128)S(1)}, f32[8,40,4]{2,1,0:T(8,128)S(1)}, u32[]{:S(2)}, u32[]{:S(2)}) %collective-permute-start.19) | collective-permute-done | bytes 5152 | tf_op jit(solution)/shard_map/ppermute | solution.py:25
  (90 shorter events, 36.8 us)
Async XLA Ops:
  6.5 12.3 %copy-start = (f32[8,32,128]{2,1,0:T(8,128)S(1)}, f32[8,32,128]{2,1,0:T(8,128)}, u32[]{:S(2)}) copy-start(f32[8,32,128]{2,1,0:T(8,128)} %param.9) | copy-start | bytes 393220
  6.5 51.5 %reduce-scatter.3.cloned.1.call-start = ((), (), s32[]{:S(2)}) async-start(), calls=%async_computation.2 | async-start | bytes 163840 | tf_op jit(solution)/shard_map/reduce_scatter | solution.py:97
  7.4 13.7 %collective-permute-start = (f32[8,4,128]{2,1,0:T(4,128)S(1)}, f32[8,4,128]{2,1,0:T(4,128)S(1)}, u32[]{:S(2)}, u32[]{:S(2)}) collective-permute-start(f32[8,4,128]{2,1,0:T(4,128)S(1)} %get-tuple-element.37), channel_id=1, source_target_pairs={{0,2},{2,4},{4,6},{6,0},{1,3},{3,5},{5,7},{7,1},{8,10},{10,12},{12... | collective-permute-start | bytes 49160 | tf_op jit(solution)/shard_map/ppermute | solution.py:23
  10.4 10.7 %collective-permute-start.1 = (f32[8,4,128]{2,1,0:T(4,128)S(1)}, f32[8,4,128]{2,1,0:T(4,128)S(1)}, u32[]{:S(2)}, u32[]{:S(2)}) collective-permute-start(f32[8,4,128]{2,1,0:T(4,128)S(1)} %get-tuple-element.38), channel_id=1, source_target_pairs={{2,0},{4,2},{6,4},{0,6},{3,1},{5,3},{7,5},{1,7},{10,8},{12,10},{14... | collective-permute-start | bytes 49160 | tf_op jit(solution)/shard_map/ppermute | solution.py:25
  13.3 5.5 %collective-permute-start.4 = (f32[8,4,128]{2,1,0:T(4,128)S(1)}, f32[8,4,128]{2,1,0:T(4,128)S(1)}, u32[]{:S(2)}, u32[]{:S(2)}) collective-permute-start(f32[8,4,128]{2,1,0:T(4,128)S(1)} %get-tuple-element.39), channel_id=1, source_target_pairs={{0,2},{2,4},{4,6},{6,0},{1,3},{3,5},{5,7},{7,1},{8,10},{10,12},{12... | collective-permute-start | bytes 49160 | tf_op jit(solution)/shard_map/ppermute | solution.py:23
  13.3 5.5 %collective-permute-start.5 = (f32[8,4,128]{2,1,0:T(4,128)S(1)}, f32[8,4,128]{2,1,0:T(4,128)S(1)}, u32[]{:S(2)}, u32[]{:S(2)}) collective-permute-start(f32[8,4,128]{2,1,0:T(4,128)S(1)} %get-tuple-element.40), channel_id=1, source_target_pairs={{2,0},{4,2},{6,4},{0,6},{3,1},{5,3},{7,5},{1,7},{10,8},{12,10},{14... | collective-permute-start | bytes 49160 | tf_op jit(solution)/shard_map/ppermute | solution.py:25
  18.8 2.2 %copy-start.1 = (f32[1,8,32,128]{3,2,1,0:T(8,128)S(1)}, f32[1,8,32,128]{3,2,1,0:T(8,128)}, u32[]{:S(2)}) copy-start(f32[1,8,32,128]{3,2,1,0:T(8,128)} %param.8) | copy-start | bytes 393220
  19.0 7.1 %collective-permute-start.6 = (f32[8,40,4]{2,1,0:T(8,128)S(1)}, f32[8,40,4]{2,1,0:T(8,128)S(1)}, u32[]{:S(2)}, u32[]{:S(2)}) collective-permute-start(f32[8,40,4]{2,1,0:T(8,128)S(1)} %get-tuple-element.29), channel_id=1, source_target_pairs={{0,1},{1,0},{2,3},{3,2},{4,5},{5,4},{6,7},{7,6},{8,9},{9,8},{10,11... | collective-permute-start | bytes 15368 | tf_op jit(solution)/shard_map/ppermute | solution.py:23
  20.7 8.9 %collective-permute-start.7 = (f32[8,40,4]{2,1,0:T(8,128)S(1)}, f32[8,40,4]{2,1,0:T(8,128)S(1)}, u32[]{:S(2)}, u32[]{:S(2)}) collective-permute-start(f32[8,40,4]{2,1,0:T(8,128)S(1)} %get-tuple-element.30), channel_id=1, source_target_pairs={{1,0},{0,1},{3,2},{2,3},{5,4},{4,5},{7,6},{6,7},{9,8},{8,9},{11,10... | collective-permute-start | bytes 15368 | tf_op jit(solution)/shard_map/ppermute | solution.py:25
  21.2 11.1 %collective-permute-start.2 = (f32[8,40,4]{2,1,0:T(8,128)S(1)}, f32[8,40,4]{2,1,0:T(8,128)S(1)}, u32[]{:S(2)}, u32[]{:S(2)}) collective-permute-start(f32[8,40,4]{2,1,0:T(8,128)S(1)} %get-tuple-element.27), channel_id=1, source_target_pairs={{0,1},{1,0},{2,3},{3,2},{4,5},{5,4},{6,7},{7,6},{8,9},{9,8},{10,11... | collective-permute-start | bytes 15368 | tf_op jit(solution)/shard_map/ppermute | solution.py:23
  22.9 11.1 %collective-permute-start.3 = (f32[8,40,4]{2,1,0:T(8,128)S(1)}, f32[8,40,4]{2,1,0:T(8,128)S(1)}, u32[]{:S(2)}, u32[]{:S(2)}) collective-permute-start(f32[8,40,4]{2,1,0:T(8,128)S(1)} %get-tuple-element.28), channel_id=1, source_target_pairs={{1,0},{0,1},{3,2},{2,3},{5,4},{4,5},{7,6},{6,7},{9,8},{8,9},{11,10... | collective-permute-start | bytes 15368 | tf_op jit(solution)/shard_map/ppermute | solution.py:25
  37.1 87.0 %reduce-scatter.5.cloned.1.call-start = ((), (), s32[]{:S(2)}) async-start(), calls=%async_computation.3 | async-start | bytes 163840 | tf_op jit(solution)/shard_map/reduce_scatter | solution.py:97
  71.4 5.6 %collective-permute-start.8 = (f32[8,4,128]{2,1,0:T(4,128)S(1)}, f32[8,4,128]{2,1,0:T(4,128)S(1)}, u32[]{:S(2)}, u32[]{:S(2)}) collective-permute-start(f32[8,4,128]{2,1,0:T(4,128)S(1)} %get-tuple-element.35), channel_id=1, source_target_pairs={{0,2},{2,4},{4,6},{6,0},{1,3},{3,5},{5,7},{7,1},{8,10},{10,12},{12... | collective-permute-start | bytes 49160 | tf_op jit(solution)/shard_map/ppermute | solution.py:23
  72.9 4.1 %collective-permute-start.9 = (f32[8,4,128]{2,1,0:T(4,128)S(1)}, f32[8,4,128]{2,1,0:T(4,128)S(1)}, u32[]{:S(2)}, u32[]{:S(2)}) collective-permute-start(f32[8,4,128]{2,1,0:T(4,128)S(1)} %get-tuple-element.36), channel_id=1, source_target_pairs={{2,0},{4,2},{6,4},{0,6},{3,1},{5,3},{7,5},{1,7},{10,8},{12,10},{14... | collective-permute-start | bytes 49160 | tf_op jit(solution)/shard_map/ppermute | solution.py:25
  77.1 7.1 %collective-permute-start.10 = (f32[8,40,4]{2,1,0:T(8,128)S(1)}, f32[8,40,4]{2,1,0:T(8,128)S(1)}, u32[]{:S(2)}, u32[]{:S(2)}) collective-permute-start(f32[8,40,4]{2,1,0:T(8,128)S(1)} %get-tuple-element.25), channel_id=1, source_target_pairs={{0,1},{1,0},{2,3},{3,2},{4,5},{5,4},{6,7},{7,6},{8,9},{9,8},{10,11... | collective-permute-start | bytes 15368 | tf_op jit(solution)/shard_map/ppermute | solution.py:23
  78.7 7.3 %collective-permute-start.11 = (f32[8,40,4]{2,1,0:T(8,128)S(1)}, f32[8,40,4]{2,1,0:T(8,128)S(1)}, u32[]{:S(2)}, u32[]{:S(2)}) collective-permute-start(f32[8,40,4]{2,1,0:T(8,128)S(1)} %get-tuple-element.26), channel_id=1, source_target_pairs={{1,0},{0,1},{3,2},{2,3},{5,4},{4,5},{7,6},{6,7},{9,8},{8,9},{11,10... | collective-permute-start | bytes 15368 | tf_op jit(solution)/shard_map/ppermute | solution.py:25
  88.3 5.6 %collective-permute-start.12 = (f32[8,4,128]{2,1,0:T(4,128)S(1)}, f32[8,4,128]{2,1,0:T(4,128)S(1)}, u32[]{:S(2)}, u32[]{:S(2)}) collective-permute-start(f32[8,4,128]{2,1,0:T(4,128)S(1)} %get-tuple-element.33), channel_id=1, source_target_pairs={{0,2},{2,4},{4,6},{6,0},{1,3},{3,5},{5,7},{7,1},{8,10},{10,12},{12... | collective-permute-start | bytes 49160 | tf_op jit(solution)/shard_map/ppermute | solution.py:23
  89.2 4.7 %collective-permute-start.13 = (f32[8,4,128]{2,1,0:T(4,128)S(1)}, f32[8,4,128]{2,1,0:T(4,128)S(1)}, u32[]{:S(2)}, u32[]{:S(2)}) collective-permute-start(f32[8,4,128]{2,1,0:T(4,128)S(1)} %get-tuple-element.34), channel_id=1, source_target_pairs={{2,0},{4,2},{6,4},{0,6},{3,1},{5,3},{7,5},{1,7},{10,8},{12,10},{14... | collective-permute-start | bytes 49160 | tf_op jit(solution)/shard_map/ppermute | solution.py:25
  94.0 5.4 %collective-permute-start.14 = (f32[8,40,4]{2,1,0:T(8,128)S(1)}, f32[8,40,4]{2,1,0:T(8,128)S(1)}, u32[]{:S(2)}, u32[]{:S(2)}) collective-permute-start(f32[8,40,4]{2,1,0:T(8,128)S(1)} %get-tuple-element.23), channel_id=1, source_target_pairs={{0,1},{1,0},{2,3},{3,2},{4,5},{5,4},{6,7},{7,6},{8,9},{9,8},{10,11... | collective-permute-start | bytes 15368 | tf_op jit(solution)/shard_map/ppermute | solution.py:23
  95.5 5.6 %collective-permute-start.15 = (f32[8,40,4]{2,1,0:T(8,128)S(1)}, f32[8,40,4]{2,1,0:T(8,128)S(1)}, u32[]{:S(2)}, u32[]{:S(2)}) collective-permute-start(f32[8,40,4]{2,1,0:T(8,128)S(1)} %get-tuple-element.24), channel_id=1, source_target_pairs={{1,0},{0,1},{3,2},{2,3},{5,4},{4,5},{7,6},{6,7},{9,8},{8,9},{11,10... | collective-permute-start | bytes 15368 | tf_op jit(solution)/shard_map/ppermute | solution.py:25
  136.9 5.6 %collective-permute-start.16 = (f32[8,4,128]{2,1,0:T(4,128)S(1)}, f32[8,4,128]{2,1,0:T(4,128)S(1)}, u32[]{:S(2)}, u32[]{:S(2)}) collective-permute-start(f32[8,4,128]{2,1,0:T(4,128)S(1)} %get-tuple-element.31), channel_id=1, source_target_pairs={{0,2},{2,4},{4,6},{6,0},{1,3},{3,5},{5,7},{7,1},{8,10},{10,12},{12... | collective-permute-start | bytes 49160 | tf_op jit(solution)/shard_map/ppermute | solution.py:23
  138.4 4.1 %collective-permute-start.17 = (f32[8,4,128]{2,1,0:T(4,128)S(1)}, f32[8,4,128]{2,1,0:T(4,128)S(1)}, u32[]{:S(2)}, u32[]{:S(2)}) collective-permute-start(f32[8,4,128]{2,1,0:T(4,128)S(1)} %get-tuple-element.32), channel_id=1, source_target_pairs={{2,0},{4,2},{6,4},{0,6},{3,1},{5,3},{7,5},{1,7},{10,8},{12,10},{14... | collective-permute-start | bytes 49160 | tf_op jit(solution)/shard_map/ppermute | solution.py:25
  142.6 7.1 %collective-permute-start.18 = (f32[8,40,4]{2,1,0:T(8,128)S(1)}, f32[8,40,4]{2,1,0:T(8,128)S(1)}, u32[]{:S(2)}, u32[]{:S(2)}) collective-permute-start(f32[8,40,4]{2,1,0:T(8,128)S(1)} %get-tuple-element.21), channel_id=1, source_target_pairs={{0,1},{1,0},{2,3},{3,2},{4,5},{5,4},{6,7},{7,6},{8,9},{9,8},{10,11... | collective-permute-start | bytes 15368 | tf_op jit(solution)/shard_map/ppermute | solution.py:23
  144.2 7.3 %collective-permute-start.19 = (f32[8,40,4]{2,1,0:T(8,128)S(1)}, f32[8,40,4]{2,1,0:T(8,128)S(1)}, u32[]{:S(2)}, u32[]{:S(2)}) collective-permute-start(f32[8,40,4]{2,1,0:T(8,128)S(1)} %get-tuple-element.22), channel_id=1, source_target_pairs={{1,0},{0,1},{3,2},{2,3},{5,4},{4,5},{7,6},{6,7},{9,8},{8,9},{11,10... | collective-permute-start | bytes 15368 | tf_op jit(solution)/shard_map/ppermute | solution.py:25
  (4 other events, 2.9 us)
Sparse Core Ops, SparseCore 0:
  37.2 20.8 reduce-scatter.2
  103.9 20.1 reduce-scatter.4
where the time goes:
time: 162 us; the launch traced here: 161 us
  waiting for transfers between devices  75.9 us (47%)
  starting transfers between devices  31.1 us (19%)
  other arithmetic  18.8 us (12%)
  between operations  14.4 us (9%)
  blocking collectives  11 us (7%)
  local copies, waits for them, and re-layouts  10.1 us (6%)
    reduce_scatter x2, waiting for transfers between devices, per_device(): lax.psum_scatter(member_term, 'mem', scatter_dimension=1, tiled=True)  40.5 us
    ppermute x10, waiting for transfers between devices, with_halo(): lax.ppermute(tail, axis, [(i, (i + 1) % count) for i in range(count)])  24.8 us
    ppermute x10, starting transfers between devices, with_halo(): lax.ppermute(head, axis, [((i + 1) % count, i) for i in range(count)])  15.9 us
    ppermute x10, starting transfers between devices, with_halo(): lax.ppermute(tail, axis, [(i, (i + 1) % count) for i in range(count)])  15.1 us
    all_gather x2, blocking collectives, per_device(): forcing = lax.all_gather(tile_field, 'mem', axis=1, tiled=True)  11 us
    ppermute x10, waiting for transfers between devices, with_halo(): lax.ppermute(head, axis, [((i + 1) % count, i) for i in range(count)])  10.5 us
    scatter-add x2, other arithmetic, per_device(): tile_field = jnp.zeros((increment.size,), jnp.float32).at[tile_cells].add...  6.56 us
    gather x2, local copies, waits for them, and re-layouts, per_device(): observed = increment.reshape(-1)[tile_cells]  6.27 us
  transfers between devices with their start and end apart: 22, of which 16 were waited for; matrix products, arithmetic and copies ran while one was open for 1% of the time, Pallas kernels for 0%

commit v1 on v0

--- a/solution.py
+++ b/solution.py
@@ -1,8 +1,11 @@
+import functools
 import math
 
 import jax
 import jax.numpy as jnp
 from jax import lax
+from jax.experimental import pallas as pl
+from jax.experimental.pallas import tpu as pltpu
 from jax.sharding import PartitionSpec as P
 
 SWEEPS = 4
@@ -113,9 +116,597 @@
     return alpha_now[None]
 
 
+LANES = 128
+SUBLANES = 8
+HALO = STEPS * SWEEPS
+SLOT = 2 * HALO
+GROUP = LANES // SLOT
+MESH = pl.DeviceIdType.MESH
+
+
+def copy_plan(members, peers, edge_tiles):
+    keys = []
+    for field in ("alpha", "kappa", "x"):
+        keys += [(field, "row", side) for side in (-1, 1)]
+    for pack in ("pack", "packx"):
+        keys += [(pack, side, peer) for side in (-1, 0, 1) for peer in range(peers)]
+    for step in range(STEPS):
+        keys += [("sum", step, hop) for hop in range(1, members)]
+        keys += [("tile", step, hop) for hop in range(1, members)]
+        keys += [("edge", step, peer, hop) for peer in range(peers) for hop in range(members)]
+    numbers = {key: number for number, key in enumerate(keys)}
+    received = len(keys)
+    for step in range(STEPS):
+        for side in (-1, 1):
+            numbers["row", step, side] = received
+            received += edge_tiles
+            for peer in range(peers):
+                numbers["corner", step, side, peer] = received
+                received += edge_tiles
+    sent = len(keys)
+    for step in range(STEPS):
+        for side in (-1, 1):
+            numbers["row_out", step, side] = sent
+            sent += members
+            for peer in range(peers):
+                numbers["corner_out", step, side, peer] = sent
+                sent += members
+    return numbers, sent, received
+
+
+def kernel(
+    members,
+    lat_count,
+    lon_count,
+    tile_rows,
+    x_ref,
+    control_ref,
+    kappa_ref,
+    cells_ref,
+    counts_ref,
+    innovations_ref,
+    precision_ref,
+    out_ref,
+    x_flat,
+    alpha_o,
+    alpha_h,
+    kappa_o,
+    kappa_h,
+    wx_o,
+    wx_h,
+    work_o,
+    work_h,
+    next_o,
+    next_h,
+    forcing_o,
+    forcing_h,
+    pack_out,
+    pack_in,
+    packx_out,
+    packx_in,
+    edge_out,
+    edge_in,
+    terms,
+    pieces,
+    tile_out,
+    rows_hot,
+    cols_hot,
+    send_sems,
+    recv_sems,
+):
+    levels = SUBLANES
+    rows = control_ref.shape[0] // levels
+    slots = cells_ref.shape[1]
+    groups = rows // GROUP
+    edge_tiles = HALO // tile_rows
+    peers = [1] if lon_count == 2 else [1, lon_count - 1]
+    numbers, _, _ = copy_plan(members, len(peers), edge_tiles)
+    weight = 1.0 / math.sqrt(members - 1)
+    mem = lax.axis_index("mem")
+    lat = lax.axis_index("lat")
+    lon = lax.axis_index("lon")
+    has = {-1: lat > 0, 0: None, 1: lat < lat_count - 1}
+
+    def guarded(condition, run):
+        if condition is None:
+            run()
+        else:
+            pl.when(condition)(run)
+
+    def device(mem_hop, lat_hop, lon_hop):
+        return (
+            lax.rem(mem + mem_hop, members),
+            lat + lat_hop,
+            lax.rem(lon + lon_hop, lon_count),
+        )
+
+    def far(peer):
+        return len(peers) - 1 - peer
+
+    def remote(src, dst, send_number, recv_number, target):
+        return pltpu.make_async_remote_copy(
+            src_ref=src,
+            dst_ref=dst,
+            send_sem=send_sems.at[send_number],
+            recv_sem=recv_sems.at[recv_number],
+            device_id=target,
+            device_id_type=MESH,
+        )
+
+    pending = []
+
+    def send(condition, src, dst, send_number, recv_number, target):
+        guarded(condition, lambda: remote(src, dst, send_number, recv_number, target).start())
+        pending.append((condition, src, send_number))
+
+    def settle(name=None):
+        kept = []
+        for condition, src, number in pending:
+            if name is None or number in (numbers[name, "row", -1], numbers[name, "row", 1]):
+                guarded(
+                    condition,
+                    lambda: remote(src, src, number, 0, device(0, 0, peers[0])).wait_send(),
+                )
+            else:
+                kept.append((condition, src, number))
+        pending[:] = kept
+
+    def await_in(condition, dst, recv_number):
+        guarded(
+            condition,
+            lambda: remote(dst, dst, 0, recv_number, device(0, 0, peers[0])).wait_recv(),
+        )
+
+    barrier = pltpu.get_barrier_semaphore()
+    for lat_hop in (0, -1, 1):
+        def greet(lat_hop=lat_hop):
+            for lon_hop in [0] + peers:
+                for mem_hop in range(members):
+                    if (lat_hop, lon_hop, mem_hop) != (0, 0, 0):
+                        pl.semaphore_signal(
+                            barrier,
+                            inc=1,
+                            device_id=device(mem_hop, lat_hop, lon_hop),
+                            device_id_type=MESH,
+                        )
+        guarded(has[lat_hop], greet)
+
+    lane = lax.broadcasted_iota(jnp.int32, (1, SUBLANES, LANES), 2)
+    lane2 = lane[0]
+
+    x_flat[...] = weight * x_ref[...].astype(jnp.float32)
+    for r in range(rows):
+        level_rows = pl.ds(r, levels, stride=rows)
+        alpha_o[HALO + r] = control_ref[level_rows, :]
+        kappa_o[HALO + r] = kappa_ref[level_rows, :]
+        wx_o[HALO + r] = x_flat[level_rows, :]
+
+    def packed(read, count):
+        total = jnp.zeros((SUBLANES, LANES), jnp.float32)
+        for j in range(count):
+            shifted = pltpu.roll(read(j), (HALO + SLOT * j) % LANES, 1)
+            total = jnp.where(lane2 // SLOT == j, shifted, total)
+        return total
+
+    def unpacked(read, j):
+        shift = (LANES - HALO - SLOT * j) % LANES
+        parts = [pltpu.roll(read(peer), shift, 1) if shift else read(peer) for peer in range(len(peers))]
+        if len(parts) == 1:
+            return parts[0]
+        return jnp.where(lane2 < LANES // 2, parts[0], parts[1])
+
+    for g in range(groups):
+        base = HALO + g * GROUP
+        pack_out[g, 0] = packed(lambda j: alpha_o[base + j], GROUP)
+        pack_out[g, 1] = packed(lambda j: kappa_o[base + j], GROUP)
+        packx_out[g] = packed(lambda j: wx_o[base + j], GROUP)
+
+    zero_rows = jnp.zeros((HALO, SUBLANES, LANES), jnp.float32)
+    for side in (-1, 1):
+        start = 0 if side < 0 else HALO + rows
+        group = 0 if side < 0 else groups + 1
+        tile = 0 if side < 0 else edge_tiles + members
+
+        def clear(start=start, group=group, tile=tile):
+            for ref in (alpha_o, kappa_o, wx_o, forcing_o.at[0], forcing_o.at[1]):
+                ref[start : start + HALO] = zero_rows
+            for peer in range(len(peers)):
+                pack_in[peer, group] = jnp.zeros((2, SUBLANES, LANES), jnp.float32)
+                packx_in[peer, group] = jnp.zeros((SUBLANES, LANES), jnp.float32)
+                for step in range(STEPS):
+                    edge_in[step, peer, tile : tile + edge_tiles] = jnp.zeros(
+                        (edge_tiles, SUBLANES, LANES), jnp.float32
+                    )
+
+        guarded(jnp.logical_not(has[side]), clear)
+
+    greeted = len(peers) + 1
+    lat_near = 1 + (lat > 0).astype(jnp.int32) + (lat < lat_count - 1).astype(jnp.int32)
+    pl.semaphore_wait(barrier, members * greeted * lat_near - 1)
+
+    def row_copies(name, field, width):
+        for side in (-1, 1):
+            source = HALO if side < 0 else HALO + rows - width
+            target = HALO + rows if side < 0 else HALO - width
+            send(
+                has[side],
+                field.at[pl.ds(source, width)],
+                field.at[pl.ds(target, width)],
+                numbers[name, "row", side],
+                numbers[name, "row", -side],
+                device(0, side, 0),
+            )
+
+    def row_waits(name, field, width):
+        for side in (-1, 1):
+            start = HALO - width if side < 0 else HALO + rows
+            await_in(has[side], field.at[pl.ds(start, width)], numbers[name, "row", side])
+
+    def pack_copies(name, source, target):
+        for side in (0, -1, 1):
+            for peer, hop in enumerate(peers):
+                if side == 0:
+                    src, dst = source, target.at[far(peer), pl.ds(1, groups)]
+                elif side < 0:
+                    src, dst = source.at[0], target.at[far(peer), groups + 1]
+                else:
+                    src, dst = source.at[groups - 1], target.at[far(peer), 0]
+                send(
+                    has[side],
+                    src,
+                    dst,
+                    numbers[name, side, peer],
+                    numbers[name, -side, far(peer)],
+                    device(0, side, hop),
+                )
+
+    def pack_waits(name, target):
+        for side in (0, -1, 1):
+            for peer in range(len(peers)):
+                if side == 0:
+                    dst = target.at[peer, pl.ds(1, groups)]
+                else:
+                    dst = target.at[peer, 0 if side < 0 else groups + 1]
+                await_in(has[side], dst, numbers[name, side, peer])
+
+    pack_copies("pack", pack_out, pack_in)
+    row_copies("alpha", alpha_o, SWEEPS)
+    row_copies("kappa", kappa_o, HALO)
+    pack_copies("packx", packx_out, packx_in)
+    row_copies("x", wx_o, HALO)
+
+    cells = cells_ref[...]
+    column = lax.rem(cells, LANES)
+    tile_row = lax.rem(lax.div(cells, LANES), tile_rows)
+    level = lax.div(cells, LANES * tile_rows)
+    place = tile_row * levels + level
+    spots = tile_rows * levels
+    rows_hot[...] = (
+        lax.broadcasted_iota(jnp.int32, (spots, slots), 0) == place
+    ).astype(jnp.float32).astype(jnp.bfloat16)
+    cols_hot[...] = (
+        lax.broadcasted_iota(jnp.int32, (LANES, slots), 0) == column
+    ).astype(jnp.float32).astype(jnp.bfloat16)
+    live = (
+        lax.broadcasted_iota(jnp.int32, (1, slots), 1) < counts_ref[0]
+    ).astype(jnp.float32)
+    masked_weight = precision_ref[...] * live
+    innovations = innovations_ref[...]
+
+    def halves(value):
+        high = value.astype(jnp.bfloat16)
+        return high, (value - high.astype(jnp.float32)).astype(jnp.bfloat16)
+
+    first_lane, last_lane = lane == 0, lane == LANES - 1
+
+    def sides(own, near):
+        own_w, near_w = pltpu.roll(own, 1, 2), pltpu.roll(near, 1, 2)
+        own_e, near_e = pltpu.roll(own, LANES - 1, 2), pltpu.roll(near, LANES - 1, 2)
+        return (
+            jnp.where(first_lane, near_w, own_w) + jnp.where(last_lane, near_e, own_e),
+            jnp.where(first_lane, own_w, near_w) + jnp.where(last_lane, own_e, near_e),
+        )
+
+    def chunks(margin):
+        first, last = HALO - margin, HALO + rows + margin
+        return [(a, min(a + 8, last)) for a in range(first, last, 8)]
+
+    def smooth_sweep(src, dst, margin, emit=None):
+        for a, b in chunks(margin):
+            own, near = src[0][a:b], src[1][a:b]
+            beside = sides(own, near)
+            for ref, value, both, kappa, out in (
+                (src[0], own, beside[0], kappa_o, dst[0]),
+                (src[1], near, beside[1], kappa_h, dst[1]),
+            ):
+                if emit is not None and ref is src[1]:
+                    continue
+                total = ref[a - 1 : b - 1] + ref[a + 1 : b + 1] + both
+                value = value + kappa[a:b] * (total - 4.0 * value)
+                if emit is None:
+                    out[a:b] = value
+                else:
+                    emit(a, b, value)
+
+    def adjoint_sweep(src, dst, margin, emit=None, near_too=True):
+        for a, b in chunks(margin):
+            scaled = [
+                kappa[a - 1 : b + 1] * ref[a - 1 : b + 1]
+                for ref, kappa in ((src[0], kappa_o), (src[1], kappa_h))
+            ]
+            beside = sides(scaled[0][1:-1], scaled[1][1:-1])
+            for which in (0, 1):
+                if which and not near_too:
+                    continue
+                t = scaled[which]
+                value = src[which][a:b] + (t[:-2] + t[2:] + beside[which] - 4.0 * t[1:-1])
+                if emit is None:
+                    dst[which][a:b] = value
+                else:
+                    emit(which, a, b, value)
+
+    work, following = (work_o, work_h), (next_o, next_h)
+
+    row_waits("alpha", alpha_o, SWEEPS)
+    row_waits("kappa", kappa_o, HALO)
+    pack_waits("pack", pack_in)
+    for e in range(rows + 2 * HALO):
+        g, j = divmod(e, GROUP)
+        alpha_h[e] = unpacked(lambda peer: pack_in[peer, g, 0], j)
+        kappa_h[e] = unpacked(lambda peer: pack_in[peer, g, 1], j)
+
+    for step in range(STEPS):
+        term = terms.at[step]
+
+        def emit_term(a, b, value):
+            term[a - HALO : b - HALO] = wx_o[a:b] * value
+
+        smooth_sweep((alpha_o, alpha_h), work, SWEEPS - 1)
+        src, dst = work, following
+        for sweep in range(1, SWEEPS):
+            last = sweep == SWEEPS - 1
+            smooth_sweep(src, dst, SWEEPS - 1 - sweep, emit_term if last else None)
+            src, dst = dst, src
+
+        for hop in range(1, members):
+            target = lax.rem(mem + hop, members)
+            send(
+                None,
+                term.at[pl.ds(target * tile_rows, tile_rows)],
+                pieces.at[step, hop],
+                numbers["sum", step, hop],
+                numbers["sum", step, hop],
+                device(hop, 0, 0),
+            )
+        total = term[pl.ds(mem * tile_rows, tile_rows)]
+        if step == 0:
+            row_waits("x", wx_o, HALO)
+            pack_waits("packx", packx_in)
+            for e in range(rows + 2 * HALO):
+                g, j = divmod(e, GROUP)
+                wx_h[e] = unpacked(lambda peer: packx_in[peer, g], j)
+        for hop in range(1, members):
+            await_in(None, pieces.at[step, hop], numbers["sum", step, hop])
+            total = total + pieces[step, hop]
+
+        flipped = jnp.transpose(total.reshape(spots, LANES))
+        hot_rows, hot_cols = rows_hot[...], cols_hot[...]
+        observed = jnp.zeros((LANES, slots), jnp.float32)
+        for half in halves(flipped):
+            observed = observed + jnp.dot(half, hot_rows, preferred_element_type=jnp.float32)
+        observed = jnp.sum(
+            observed * hot_cols.astype(jnp.float32), axis=0, keepdims=True
+        )
+        misfit = (observed - innovations) * masked_weight
+        pulled = jnp.clip(misfit, -huber_edge, huber_edge) * masked_weight
+        tile = jnp.zeros((spots, LANES), jnp.float32)
+        for half in halves(pulled):
+            tile = tile + lax.dot_general(
+                hot_rows * half,
+                hot_cols,
+                (((1,), (1,)), ((), ())),
+                preferred_element_type=jnp.float32,
+            )
+        tile = tile.reshape(tile_rows, SUBLANES, LANES)
+        tile_out[step] = tile
+        edge_out[step] = packed(lambda j: tile[j], tile_rows)
+
+        force_o, edges = forcing_o.at[step], edge_in.at[step]
+        for hop in range(1, members):
+            send(
+                None,
+                tile_out.at[step],
+                force_o.at[pl.ds(HALO + mem * tile_rows, tile_rows)],
+                numbers["tile", step, hop],
+                numbers["tile", step, hop],
+                device(hop, 0, 0),
+            )
+        for side in (-1, 1):
+            near = mem - (0 if side < 0 else members - edge_tiles)
+            inside = near < edge_tiles if side < 0 else near >= 0
+            condition = jnp.logical_and(has[side], inside)
+            row = near * tile_rows + (HALO + rows if side < 0 else 0)
+            spot = near + (edge_tiles + members if side < 0 else 0)
+            for hop in range(members):
+                send(
+                    condition,
+                    tile_out.at[step],
+                    force_o.at[pl.ds(row, tile_rows)],
+                    numbers["row_out", step, side] + hop,
+                    numbers["row", step, -side] + near,
+                    device(hop, side, 0),
+                )
+            for peer, lon_hop in enumerate(peers):
+                for hop in range(members):
+                    send(
+                        condition,
+                        edge_out.at[step],
+                        edges.at[far(peer), spot],
+                        numbers["corner_out", step, side, peer] + hop,
+                        numbers["corner", step, -side, far(peer)] + near,
+                        device(hop, side, lon_hop),
+                    )
+        for peer, lon_hop in enumerate(peers):
+            for hop in range(members):
+                send(
+                    None,
+                    edge_out.at[step],
+                    edges.at[far(peer), edge_tiles + mem],
+                    numbers["edge", step, peer, hop],
+                    numbers["edge", step, far(peer), hop],
+                    device(hop, 0, lon_hop),
+                )
+        force_o[pl.ds(HALO + mem * tile_rows, tile_rows)] = tile
+
+        for hop in range(1, members):
+            source = lax.rem(mem + members - hop, members)
+            await_in(
+                None,
+                force_o.at[pl.ds(HALO + source * tile_rows, tile_rows)],
+                numbers["tile", step, hop],
+            )
+        for peer in range(len(peers)):
+            for hop in range(members):
+                source = lax.rem(mem + members - hop, members)
+                await_in(
+                    None, edges.at[peer, edge_tiles + source], numbers["edge", step, peer, hop]
+                )
+        for side in (-1, 1):
+            for i in range(edge_tiles):
+                row = i * tile_rows + (0 if side < 0 else HALO + rows)
+                spot = i + (0 if side < 0 else edge_tiles + members)
+                await_in(
+                    has[side],
+                    force_o.at[pl.ds(row, tile_rows)],
+                    numbers["row", step, side] + i,
+                )
+                for peer in range(len(peers)):
+                    await_in(
+                        has[side],
+                        edges.at[peer, spot],
+                        numbers["corner", step, side, peer] + i,
+                    )
+
+        margin = HALO - step * SWEEPS
+        for e in range(HALO - margin, HALO + rows + margin):
+            t, j = divmod(e, tile_rows)
+            forcing_h[e] = unpacked(lambda peer: edges[peer, t], j)
+        for a, b in chunks(margin):
+            work_o[a:b] = wx_o[a:b] * force_o[a:b]
+            work_h[a:b] = wx_h[a:b] * forcing_h[a:b]
+
+        final = step == STEPS - 1
+        inside_top = (lat > 0).astype(jnp.float32)
+        inside_bottom = (lat < lat_count - 1).astype(jnp.float32)
+
+        def emit_alpha(which, a, b, value):
+            held = (alpha_o, alpha_h)[which]
+            old = held[a:b]
+            fresh = old - step_length * (old + value)
+            if final:
+                for r in range(a, b):
+                    out_ref[pl.ds(r - HALO, levels, stride=rows), :] = fresh[r - a]
+                return
+            for r in range(a, b):
+                row = fresh[r - a]
+                if r < HALO:
+                    row = row * inside_top
+                elif r >= HALO + rows:
+                    row = row * inside_bottom
+                held[r] = row
+
+        if step == 0:
+            settle("alpha")
+        src, dst = work, following
+        for sweep in range(SWEEPS):
+            last = sweep == SWEEPS - 1
+            adjoint_sweep(
+                src, dst, margin - 1 - sweep, emit_alpha if last else None, not (last and final)
+            )
+            src, dst = dst, src
+
+    settle()
+
+
+def fused(members, lat_count, lon_count, tile_rows, x, control, kappa, cells, counts, innov, prec):
+    _, levels, rows, columns = x.shape
+    peers = 1 if lon_count == 2 else 2
+    edge_tiles = HALO // tile_rows
+    slots = cells.shape[1]
+    groups = rows // GROUP
+    _, sent, received = copy_plan(members, peers, edge_tiles)
+    vregs = lambda *lead: pltpu.VMEM(lead + (SUBLANES, LANES), jnp.float32)
+    deep = rows + 2 * HALO
+    tiles = members + 2 * edge_tiles
+    vmem = pl.BlockSpec(memory_space=pltpu.VMEM)
+    out = pl.pallas_call(
+        functools.partial(kernel, members, lat_count, lon_count, tile_rows),
+        out_shape=jax.ShapeDtypeStruct((levels * rows, columns), jnp.float32),
+        in_specs=[vmem] * 4 + [pl.BlockSpec(memory_space=pltpu.SMEM)] + [vmem] * 2,
+        out_specs=vmem,
+        scratch_shapes=[pltpu.VMEM((levels * rows, columns), jnp.float32)]
+        + [vregs(deep)] * 10
+        + [
+            vregs(STEPS, deep),
+            vregs(deep),
+            vregs(groups, 2),
+            vregs(peers, groups + 2, 2),
+            vregs(groups),
+            vregs(peers, groups + 2),
+            vregs(STEPS),
+            vregs(STEPS, peers, tiles),
+            vregs(STEPS, rows),
+            vregs(STEPS, members, tile_rows),
+            vregs(STEPS, tile_rows),
+            pltpu.VMEM((tile_rows * levels, slots), jnp.bfloat16),
+            pltpu.VMEM((LANES, slots), jnp.bfloat16),
+            pltpu.SemaphoreType.DMA((sent,)),
+            pltpu.SemaphoreType.DMA((received,)),
+        ],
+        compiler_params=pltpu.CompilerParams(collective_id=0, has_side_effects=True),
+    )(
+        x.reshape(levels * rows, columns),
+        control.reshape(levels * rows, columns),
+        kappa.reshape(levels * rows, columns),
+        cells,
+        counts,
+        innov,
+        prec,
+    )
+    return out.reshape(1, levels, rows, columns)
+
+
+def fits(members, lat_count, lon_count, x, cells):
+    _, levels, rows, columns = x.shape
+    tile_rows = rows // members
+    return (
+        levels == SUBLANES
+        and columns == LANES
+        and rows % members == 0
+        and rows % GROUP == 0
+        and rows >= 2 * HALO
+        and HALO % tile_rows == 0
+        and tile_rows <= GROUP
+        and HALO // tile_rows <= members
+        and lon_count > 1
+        and cells.shape[0] == 1
+    )
+
+
+def on_device(members, lat_count, lon_count, x, control, kappa, cells, counts, innov, prec):
+    if not fits(members, lat_count, lon_count, x, cells):
+        return per_device(x, control, kappa, cells, counts, innov, prec)
+    tile_rows = x.shape[2] // members
+    return fused(
+        members, lat_count, lon_count, tile_rows, x, control, kappa, cells, counts, innov, prec
+    )
+
+
 def solution(mesh):
     return jax.shard_map(
-        per_device,
+        functools.partial(
+            on_device, mesh.shape["mem"], mesh.shape["lat"], mesh.shape["lon"]
+        ),
         mesh=mesh,
         in_specs=(
             P("mem", None, "lat", "lon"),

time: 162 us -> 33.5 us (0.21)
  waiting for transfers between devices: 75.9 us -> 0 us
  Pallas kernels: 0 us -> 31.1 us
  starting transfers between devices: 31.1 us -> 0 us
  other arithmetic: 18.8 us -> 0 us
  between operations: 14.4 us -> 0.66 us
  blocking collectives: 11 us -> 0 us
  local copies, waits for them, and re-layouts: 10.1 us -> 1.57 us
    reduce_scatter x2 -> x0, waiting for transfers between devices: 40.5 us -> none  [per_device(): lax.psum_scatter(member_term, 'mem', scatter_dimension=1, tiled=True)]
    ppermute x20 -> x0, waiting for transfers between devices: 35.3 us -> none  [the longest x10 24.8 us: with_halo(): lax.ppermute(tail, axis, [(i, (i + 1) % count) for i in range(count)])]
    pallas_call x0 -> x1, Pallas kernels: none -> 31.1 us  [fused(): pl.pallas_call(functools.partial(kernel, members, lat_count, lon_count, t...]
    ppermute x20 -> x0, starting transfers between devices: 31 us -> none  [the longest x10 15.9 us: with_halo(): lax.ppermute(head, axis, [((i + 1) % count, i) for i in range(count)])]
    all_gather x2 -> x0, blocking collectives: 11 us -> none  [per_device(): forcing = lax.all_gather(tile_field, 'mem', axis=1, tiled=True)]
    mul x23 -> x0, other arithmetic: 9.23 us -> none  [the longest x8 3.96 us: adjoint_deep(): laplace_term, center = stencil(local_kappa * padded)]
    scatter-add x2 -> x0, other arithmetic: 6.56 us -> none  [per_device(): tile_field = jnp.zeros((increment.size,), jnp.float32).at[tile_cells].add...]
    gather x2 -> x0, local copies, waits for them, and re-layouts: 6.27 us -> none  [per_device(): observed = increment.reshape(-1)[tile_cells]]
  transfers between devices with their start and end apart: 22 -> 0, of which waited for: 16 -> 0; matrix products, arithmetic and copies ran while one was open for 1% -> 0% of each run, Pallas kernels for 0% -> 0%
where the time goes in v1:
time: 33.5 us; the launch traced here: 33.3 us
  Pallas kernels  31.1 us (93%)
  local copies, waits for them, and re-layouts  1.57 us (5%)
  between operations  0.66 us (2%)
    pallas_call x1, Pallas kernels, fused(): pl.pallas_call(functools.partial(kernel, members, lat_count, lon_count, t...  31.1 us
    unnamed x1, local copies, waits for them, and re-layouts  1.57 us

profile of v1, /device:TPU:0, one launch (start us, length us, event | category | flops | bytes accessed | tf_op | source)
XLA Modules:
  0.0 33.3 jit_solution(18068684143255065743)
XLA Ops:
  0.7 31.1 %shard_map.73 = f32[256,128]{1,0:T(8,128)} custom-call(bf16[256,128]{1,0:T(8,128)(2,1)} %bitcast.7, f32[256,128]{1,0:T(8,128)} %bitcast.5, f32[256,128]{1,0:T(8,128)} %bitcast.6, s32[1,512]{1,0:T(1,128)} %cells_ref.1, s32[1]{0:T(128)S(6)} %copy.9.counts_ref, f32[1,512]{1,0:T(1,128)} %innovations_ref.1, f32[1,512]{1,0:T(1,128)} %precision_ref.1), custom_call_target="tpu_custom_call" | custom-call | tf_op jit(solution)/shard_map/pallas_call | solution.py:642
  31.7 1.6 %copy.10 = f32[1,8,32,128]{3,2,1,0:T(8,128)} copy(f32[1,8,32,128]{3,2,1,0:T(8,128)} %bitcast.4) | data formatting | bytes 262144

commit v2 on v1

--- a/solution.py
+++ b/solution.py
@@ -126,7 +126,7 @@
 
 def copy_plan(members, peers, edge_tiles):
     keys = []
-    for field in ("alpha", "kappa", "x"):
+    for field in ("alpha", "kappa", "kappa_far", "x"):
         keys += [(field, "row", side) for side in (-1, 1)]
     for pack in ("pack", "packx"):
         keys += [(pack, side, peer) for side in (-1, 0, 1) for peer in range(peers)]
@@ -159,14 +159,21 @@
     lat_count,
     lon_count,
     tile_rows,
+    x_in,
+    control_in,
+    kappa_in,
+    cells_in,
+    counts_ref,
+    innovations_in,
+    precision_in,
+    out_ref,
     x_ref,
     control_ref,
     kappa_ref,
     cells_ref,
-    counts_ref,
     innovations_ref,
     precision_ref,
-    out_ref,
+    load_sems,
     x_flat,
     alpha_o,
     alpha_h,
@@ -257,6 +264,22 @@
             lambda: remote(dst, dst, 0, recv_number, device(0, 0, peers[0])).wait_recv(),
         )
 
+    loads = [
+        pltpu.make_async_copy(src, dst, load_sems.at[number])
+        for number, (src, dst) in enumerate(
+            (
+                (control_in, control_ref),
+                (kappa_in, kappa_ref),
+                (x_in, x_ref),
+                (cells_in, cells_ref),
+                (innovations_in, innovations_ref),
+                (precision_in, precision_ref),
+            )
+        )
+    ]
+    for load in loads:
+        load.start()
+
     barrier = pltpu.get_barrier_semaphore()
     for lat_hop in (0, -1, 1):
         def greet(lat_hop=lat_hop):
@@ -274,6 +297,8 @@
     lane = lax.broadcasted_iota(jnp.int32, (1, SUBLANES, LANES), 2)
     lane2 = lane[0]
 
+    for load in loads:
+        load.wait()
     x_flat[...] = weight * x_ref[...].astype(jnp.float32)
     for r in range(rows):
         level_rows = pl.ds(r, levels, stride=rows)
@@ -324,10 +349,10 @@
     lat_near = 1 + (lat > 0).astype(jnp.int32) + (lat < lat_count - 1).astype(jnp.int32)
     pl.semaphore_wait(barrier, members * greeted * lat_near - 1)
 
-    def row_copies(name, field, width):
+    def row_copies(name, field, width, skip=0):
         for side in (-1, 1):
-            source = HALO if side < 0 else HALO + rows - width
-            target = HALO + rows if side < 0 else HALO - width
+            source = HALO + skip if side < 0 else HALO + rows - width - skip
+            target = HALO + rows + skip if side < 0 else HALO - width - skip
             send(
                 has[side],
                 field.at[pl.ds(source, width)],
@@ -337,9 +362,9 @@
                 device(0, side, 0),
             )
 
-    def row_waits(name, field, width):
+    def row_waits(name, field, width, skip=0):
         for side in (-1, 1):
-            start = HALO - width if side < 0 else HALO + rows
+            start = HALO - width - skip if side < 0 else HALO + rows + skip
             await_in(has[side], field.at[pl.ds(start, width)], numbers[name, "row", side])
 
     def pack_copies(name, source, target):
@@ -371,8 +396,9 @@
 
     pack_copies("pack", pack_out, pack_in)
     row_copies("alpha", alpha_o, SWEEPS)
-    row_copies("kappa", kappa_o, HALO)
+    row_copies("kappa", kappa_o, SWEEPS)
     pack_copies("packx", packx_out, packx_in)
+    row_copies("kappa_far", kappa_o, HALO - SWEEPS, SWEEPS)
     row_copies("x", wx_o, HALO)
 
     cells = cells_ref[...]
@@ -448,7 +474,7 @@
     work, following = (work_o, work_h), (next_o, next_h)
 
     row_waits("alpha", alpha_o, SWEEPS)
-    row_waits("kappa", kappa_o, HALO)
+    row_waits("kappa", kappa_o, SWEEPS)
     pack_waits("pack", pack_in)
     for e in range(rows + 2 * HALO):
         g, j = divmod(e, GROUP)
@@ -480,6 +506,7 @@
             )
         total = term[pl.ds(mem * tile_rows, tile_rows)]
         if step == 0:
+            row_waits("kappa_far", kappa_o, HALO - SWEEPS, SWEEPS)
             row_waits("x", wx_o, HALO)
             pack_waits("packx", packx_in)
             for e in range(rows + 2 * HALO):
@@ -602,11 +629,12 @@
         def emit_alpha(which, a, b, value):
             held = (alpha_o, alpha_h)[which]
             old = held[a:b]
-            fresh = old - step_length * (old + value)
             if final:
+                fresh = ((1.0 - step_length) / step_length) * old - value
                 for r in range(a, b):
                     out_ref[pl.ds(r - HALO, levels, stride=rows), :] = fresh[r - a]
                 return
+            fresh = old - step_length * (old + value)
             for r in range(a, b):
                 row = fresh[r - a]
                 if r < HALO:
@@ -639,12 +667,23 @@
     deep = rows + 2 * HALO
     tiles = members + 2 * edge_tiles
     vmem = pl.BlockSpec(memory_space=pltpu.VMEM)
+    place = pl.BlockSpec(memory_space=pl.ANY)
+    flat = lambda dtype: pltpu.VMEM((levels * rows, columns), dtype)
     out = pl.pallas_call(
         functools.partial(kernel, members, lat_count, lon_count, tile_rows),
         out_shape=jax.ShapeDtypeStruct((levels * rows, columns), jnp.float32),
-        in_specs=[vmem] * 4 + [pl.BlockSpec(memory_space=pltpu.SMEM)] + [vmem] * 2,
+        in_specs=[place] * 4 + [pl.BlockSpec(memory_space=pltpu.SMEM)] + [place] * 2,
         out_specs=vmem,
-        scratch_shapes=[pltpu.VMEM((levels * rows, columns), jnp.float32)]
+        scratch_shapes=[
+            flat(x.dtype),
+            flat(jnp.float32),
+            flat(jnp.float32),
+            pltpu.VMEM(cells.shape, cells.dtype),
+            pltpu.VMEM(innov.shape, innov.dtype),
+            pltpu.VMEM(prec.shape, prec.dtype),
+            pltpu.SemaphoreType.DMA((6,)),
+            flat(jnp.float32),
+        ]
         + [vregs(deep)] * 10
         + [
             vregs(STEPS, deep),
@@ -673,7 +712,7 @@
         innov,
         prec,
     )
-    return out.reshape(1, levels, rows, columns)
+    return (step_length * out).reshape(1, levels, rows, columns)
 
 
 def fits(members, lat_count, lon_count, x, cells):

time: 33.5 us -> 32.4 us (0.967)
  other arithmetic: 0 us -> 1.57 us
  local copies, waits for them, and re-layouts: 1.57 us -> 0 us
  Pallas kernels: 31.1 us -> 30 us
    mul x0 -> x1, other arithmetic: none -> 1.57 us  [fused(): return (step_length * out).reshape(1, levels, rows, columns)]
    unnamed x1 -> x0, local copies, waits for them, and re-layouts: 1.57 us -> none
    pallas_call x1, Pallas kernels: 31.1 us -> 30 us  [fused(): pl.pallas_call(functools.partial(kernel, members, lat_count, lon_count, t...]
where the time goes in v2:
time: 32.4 us; the launch traced here: 32.3 us
  Pallas kernels  30 us (93%)
  other arithmetic  1.57 us (5%)
  between operations  0.66 us (2%)
    pallas_call x1, Pallas kernels, fused(): pl.pallas_call(functools.partial(kernel, members, lat_count, lon_count, t...  30 us
    mul x1, other arithmetic, fused(): return (step_length * out).reshape(1, levels, rows, columns)  1.57 us

profile of v2, /device:TPU:0, one launch (start us, length us, event | category | flops | bytes accessed | tf_op | source)
XLA Modules:
  0.0 32.3 jit_solution(5334766765674794211)
XLA Ops:
  0.7 30.0 %shard_map.73 = f32[256,128]{1,0:T(8,128)} custom-call(bf16[256,128]{1,0:T(8,128)(2,1)} %bitcast.6, f32[256,128]{1,0:T(8,128)} %bitcast.4, f32[256,128]{1,0:T(8,128)} %bitcast.5, s32[1,512]{1,0:T(1,128)} %cells_in.1, s32[1]{0:T(128)S(6)} %copy.8.counts_ref, f32[1,512]{1,0:T(1,128)} %innovations_in.1, f32[1,512]{1,0:T(1,128)} %precision_in.1), custom_call_target="tpu_custom_call" | custom-call | tf_op jit(solution)/shard_map/pallas_call | solution.py:672
  30.7 1.6 %broadcast_multiply_fusion = f32[256,128]{1,0:T(8,128)} fusion(f32[256,128]{1,0:T(8,128)} %shard_map.73), kind=kLoop, calls=%fused_computation | loop fusion | flops 32768 | bytes 262144 | tf_op jit(solution)/shard_map/mul | solution.py:715

commit v3 on v2

--- a/solution.py
+++ b/solution.py
@@ -130,12 +130,16 @@
         keys += [(field, "row", side) for side in (-1, 1)]
     for pack in ("pack", "packx"):
         keys += [(pack, side, peer) for side in (-1, 0, 1) for peer in range(peers)]
+    keys += [("cells", hop) for hop in range(1, members)]
     for step in range(STEPS):
         keys += [("sum", step, hop) for hop in range(1, members)]
         keys += [("tile", step, hop) for hop in range(1, members)]
         keys += [("edge", step, peer, hop) for peer in range(peers) for hop in range(members)]
     numbers = {key: number for number, key in enumerate(keys)}
     received = len(keys)
+    for side in (-1, 1):
+        numbers["cells_row", side] = received
+        received += edge_tiles
     for step in range(STEPS):
         for side in (-1, 1):
             numbers["row", step, side] = received
@@ -144,6 +148,9 @@
                 numbers["corner", step, side, peer] = received
                 received += edge_tiles
     sent = len(keys)
+    for side in (-1, 1):
+        numbers["cells_out", side] = sent
+        sent += members
     for step in range(STEPS):
         for side in (-1, 1):
             numbers["row_out", step, side] = sent
@@ -195,7 +202,9 @@
     edge_in,
     terms,
     pieces,
-    tile_out,
+    pulled_out,
+    pulled_in,
+    cells_all,
     rows_hot,
     cols_hot,
     send_sems,
@@ -333,8 +342,13 @@
         tile = 0 if side < 0 else edge_tiles + members
 
         def clear(start=start, group=group, tile=tile):
-            for ref in (alpha_o, kappa_o, wx_o, forcing_o.at[0], forcing_o.at[1]):
+            for ref in (alpha_o, kappa_o, wx_o):
                 ref[start : start + HALO] = zero_rows
+            cells_all[tile : tile + edge_tiles] = jnp.zeros((edge_tiles, 1, slots), jnp.int32)
+            for step in range(STEPS):
+                pulled_in[step, tile : tile + edge_tiles] = jnp.zeros(
+                    (edge_tiles, 1, slots), jnp.float32
+                )
             for peer in range(len(peers)):
                 pack_in[peer, group] = jnp.zeros((2, SUBLANES, LANES), jnp.float32)
                 packx_in[peer, group] = jnp.zeros((SUBLANES, LANES), jnp.float32)
@@ -401,18 +415,67 @@
     row_copies("kappa_far", kappa_o, HALO - SWEEPS, SWEEPS)
     row_copies("x", wx_o, HALO)
 
-    cells = cells_ref[...]
-    column = lax.rem(cells, LANES)
-    tile_row = lax.rem(lax.div(cells, LANES), tile_rows)
-    level = lax.div(cells, LANES * tile_rows)
-    place = tile_row * levels + level
+    def to_group(step, source, target, name):
+        for hop in range(1, members):
+            send(
+                None,
+                source,
+                target.at[edge_tiles + mem],
+                numbers[name + (hop,)],
+                numbers[name + (hop,)],
+                device(hop, 0, 0),
+            )
+        outs, ins = ("cells_out", "cells_row") if step is None else ("row_out", "row")
+        key = () if step is None else (step,)
+        for side in (-1, 1):
+            near = mem - (0 if side < 0 else members - edge_tiles)
+            inside = near < edge_tiles if side < 0 else near >= 0
+            for hop in range(members):
+                send(
+                    jnp.logical_and(has[side], inside),
+                    source,
+                    target.at[near + (edge_tiles + members if side < 0 else 0)],
+                    numbers[(outs,) + key + (side,)] + hop,
+                    numbers[(ins,) + key + (-side,)] + near,
+                    device(hop, side, 0),
+                )
+
+    def others():
+        for hop in range(1, members):
+            yield None, hop, edge_tiles + lax.rem(mem + members - hop, members)
+        for side in (-1, 1):
+            for i in range(edge_tiles):
+                yield side, i, i + (0 if side < 0 else edge_tiles + members)
+
+    to_group(None, cells_ref, cells_all, ("cells",))
+
     spots = tile_rows * levels
-    rows_hot[...] = (
-        lax.broadcasted_iota(jnp.int32, (spots, slots), 0) == place
-    ).astype(jnp.float32).astype(jnp.bfloat16)
-    cols_hot[...] = (
-        lax.broadcasted_iota(jnp.int32, (LANES, slots), 0) == column
-    ).astype(jnp.float32).astype(jnp.bfloat16)
+
+    def hot(spot, cells):
+        column = lax.rem(cells, LANES)
+        tile_row = lax.rem(lax.div(cells, LANES), tile_rows)
+        level = lax.div(cells, LANES * tile_rows)
+        place = tile_row * levels + level
+        rows_hot[spot] = (
+            lax.broadcasted_iota(jnp.int32, (spots, slots), 0) == place
+        ).astype(jnp.float32).astype(jnp.bfloat16)
+        cols_hot[spot] = (
+            lax.broadcasted_iota(jnp.int32, (LANES, slots), 0) == column
+        ).astype(jnp.float32).astype(jnp.bfloat16)
+
+    def spread(spot, pulled):
+        tile = jnp.zeros((spots, LANES), jnp.float32)
+        for half in halves(pulled):
+            tile = tile + lax.dot_general(
+                rows_hot[spot] * half,
+                cols_hot[spot],
+                (((1,), (1,)), ((), ())),
+                preferred_element_type=jnp.float32,
+            )
+        return tile.reshape(tile_rows, SUBLANES, LANES)
+
+    mine = edge_tiles + mem
+    hot(mine, cells_ref[...])
     live = (
         lax.broadcasted_iota(jnp.int32, (1, slots), 1) < counts_ref[0]
     ).astype(jnp.float32)
@@ -512,12 +575,19 @@
             for e in range(rows + 2 * HALO):
                 g, j = divmod(e, GROUP)
                 wx_h[e] = unpacked(lambda peer: packx_in[peer, g], j)
+            for side, i, spot in others():
+                if side is None:
+                    await_in(None, cells_all.at[spot], numbers["cells", i])
+                else:
+                    await_in(has[side], cells_all.at[spot], numbers["cells_row", side] + i)
+            for _, _, spot in others():
+                hot(spot, cells_all[spot])
         for hop in range(1, members):
             await_in(None, pieces.at[step, hop], numbers["sum", step, hop])
             total = total + pieces[step, hop]
 
         flipped = jnp.transpose(total.reshape(spots, LANES))
-        hot_rows, hot_cols = rows_hot[...], cols_hot[...]
+        hot_rows, hot_cols = rows_hot[mine], cols_hot[mine]
         observed = jnp.zeros((LANES, slots), jnp.float32)
         for half in halves(flipped):
             observed = observed + jnp.dot(half, hot_rows, preferred_element_type=jnp.float32)
@@ -526,43 +596,17 @@
         )
         misfit = (observed - innovations) * masked_weight
         pulled = jnp.clip(misfit, -huber_edge, huber_edge) * masked_weight
-        tile = jnp.zeros((spots, LANES), jnp.float32)
-        for half in halves(pulled):
-            tile = tile + lax.dot_general(
-                hot_rows * half,
-                hot_cols,
-                (((1,), (1,)), ((), ())),
-                preferred_element_type=jnp.float32,
-            )
-        tile = tile.reshape(tile_rows, SUBLANES, LANES)
-        tile_out[step] = tile
+        pulled_out[step] = pulled
+        to_group(step, pulled_out.at[step], pulled_in.at[step], ("tile", step))
+        tile = spread(mine, pulled)
         edge_out[step] = packed(lambda j: tile[j], tile_rows)
 
         force_o, edges = forcing_o.at[step], edge_in.at[step]
-        for hop in range(1, members):
-            send(
-                None,
-                tile_out.at[step],
-                force_o.at[pl.ds(HALO + mem * tile_rows, tile_rows)],
-                numbers["tile", step, hop],
-                numbers["tile", step, hop],
-                device(hop, 0, 0),
-            )
         for side in (-1, 1):
             near = mem - (0 if side < 0 else members - edge_tiles)
             inside = near < edge_tiles if side < 0 else near >= 0
             condition = jnp.logical_and(has[side], inside)
-            row = near * tile_rows + (HALO + rows if side < 0 else 0)
             spot = near + (edge_tiles + members if side < 0 else 0)
-            for hop in range(members):
-                send(
-                    condition,
-                    tile_out.at[step],
-                    force_o.at[pl.ds(row, tile_rows)],
-                    numbers["row_out", step, side] + hop,
-                    numbers["row", step, -side] + near,
-                    device(hop, side, 0),
-                )
             for peer, lon_hop in enumerate(peers):
                 for hop in range(members):
                     send(
@@ -585,13 +629,13 @@
                 )
         force_o[pl.ds(HALO + mem * tile_rows, tile_rows)] = tile
 
-        for hop in range(1, members):
-            source = lax.rem(mem + members - hop, members)
-            await_in(
-                None,
-                force_o.at[pl.ds(HALO + source * tile_rows, tile_rows)],
-                numbers["tile", step, hop],
-            )
+        for side, i, spot in others():
+            if side is None:
+                await_in(None, pulled_in.at[step, spot], numbers["tile", step, i])
+            else:
+                await_in(has[side], pulled_in.at[step, spot], numbers["row", step, side] + i)
+        for _, _, spot in others():
+            force_o[pl.ds(spot * tile_rows, tile_rows)] = spread(spot, pulled_in[step, spot])
         for peer in range(len(peers)):
             for hop in range(members):
                 source = lax.rem(mem + members - hop, members)
@@ -600,13 +644,7 @@
                 )
         for side in (-1, 1):
             for i in range(edge_tiles):
-                row = i * tile_rows + (0 if side < 0 else HALO + rows)
                 spot = i + (0 if side < 0 else edge_tiles + members)
-                await_in(
-                    has[side],
-                    force_o.at[pl.ds(row, tile_rows)],
-                    numbers["row", step, side] + i,
-                )
                 for peer in range(len(peers)):
                     await_in(
                         has[side],
@@ -696,9 +734,11 @@
             vregs(STEPS, peers, tiles),
             vregs(STEPS, rows),
             vregs(STEPS, members, tile_rows),
-            vregs(STEPS, tile_rows),
-            pltpu.VMEM((tile_rows * levels, slots), jnp.bfloat16),
-            pltpu.VMEM((LANES, slots), jnp.bfloat16),
+            pltpu.VMEM((STEPS, 1, slots), jnp.float32),
+            pltpu.VMEM((STEPS, tiles, 1, slots), jnp.float32),
+            pltpu.VMEM((tiles, 1, slots), jnp.int32),
+            pltpu.VMEM((tiles, tile_rows * levels, slots), jnp.bfloat16),
+            pltpu.VMEM((tiles, LANES, slots), jnp.bfloat16),
             pltpu.SemaphoreType.DMA((sent,)),
             pltpu.SemaphoreType.DMA((received,)),
         ],

time: 32.4 us -> 30.2 us (0.932)
  Pallas kernels: 30 us -> 27.8 us
    pallas_call x1, Pallas kernels: 30 us -> 27.8 us  [fused(): pl.pallas_call(functools.partial(kernel, members, lat_count, lon_count, t...]
where the time goes in v3:
time: 30.2 us; the launch traced here: 30 us
  Pallas kernels  27.8 us (92%)
  other arithmetic  1.57 us (5%)
  between operations  0.66 us (2%)
    pallas_call x1, Pallas kernels, fused(): pl.pallas_call(functools.partial(kernel, members, lat_count, lon_count, t...  27.8 us
    mul x1, other arithmetic, fused(): return (step_length * out).reshape(1, levels, rows, columns)  1.57 us

profile of v3, /device:TPU:0, one launch (start us, length us, event | category | flops | bytes accessed | tf_op | source)
XLA Modules:
  0.0 30.0 jit_solution(15971751095821109221)
XLA Ops:
  0.7 27.8 %shard_map.73 = f32[256,128]{1,0:T(8,128)} custom-call(bf16[256,128]{1,0:T(8,128)(2,1)} %bitcast.6, f32[256,128]{1,0:T(8,128)} %bitcast.4, f32[256,128]{1,0:T(8,128)} %bitcast.5, s32[1,512]{1,0:T(1,128)} %cells_in.1, s32[1]{0:T(128)S(6)} %copy.8.counts_ref, f32[1,512]{1,0:T(1,128)} %innovations_in.1, f32[1,512]{1,0:T(1,128)} %precision_in.1), custom_call_target="tpu_custom_call" | custom-call | tf_op jit(solution)/shard_map/pallas_call | solution.py:710
  28.4 1.6 %broadcast_multiply_fusion = f32[256,128]{1,0:T(8,128)} fusion(f32[256,128]{1,0:T(8,128)} %shard_map.73), kind=kLoop, calls=%fused_computation | loop fusion | flops 32768 | bytes 262144 | tf_op jit(solution)/shard_map/mul | solution.py:755

commit v4 on v3

--- a/solution.py
+++ b/solution.py
@@ -293,7 +293,7 @@
     for lat_hop in (0, -1, 1):
         def greet(lat_hop=lat_hop):
             for lon_hop in [0] + peers:
-                for mem_hop in range(members):
+                for mem_hop in range(members if lon_hop == 0 else 1):
                     if (lat_hop, lon_hop, mem_hop) != (0, 0, 0):
                         pl.semaphore_signal(
                             barrier,
@@ -359,9 +359,9 @@
 
         guarded(jnp.logical_not(has[side]), clear)
 
-    greeted = len(peers) + 1
+    greeted = len(peers) + members
     lat_near = 1 + (lat > 0).astype(jnp.int32) + (lat < lat_count - 1).astype(jnp.int32)
-    pl.semaphore_wait(barrier, members * greeted * lat_near - 1)
+    pl.semaphore_wait(barrier, greeted * lat_near - 1)
 
     def row_copies(name, field, width, skip=0):
         for side in (-1, 1):

time: 30.2 us -> 29.9 us (0.990)
  no operation moved by 1% of the time
where the time goes in v4:
time: 29.9 us; the launch traced here: 29.8 us
  Pallas kernels  27.5 us (92%)
  other arithmetic  1.57 us (5%)
  between operations  0.66 us (2%)
    pallas_call x1, Pallas kernels, fused(): pl.pallas_call(functools.partial(kernel, members, lat_count, lon_count, t...  27.5 us
    mul x1, other arithmetic, fused(): return (step_length * out).reshape(1, levels, rows, columns)  1.57 us

profile of v4, /device:TPU:0, one launch (start us, length us, event | category | flops | bytes accessed | tf_op | source)
XLA Modules:
  0.0 29.8 jit_solution(7977165345053630349)
XLA Ops:
  0.7 27.5 %shard_map.73 = f32[256,128]{1,0:T(8,128)} custom-call(bf16[256,128]{1,0:T(8,128)(2,1)} %bitcast.6, f32[256,128]{1,0:T(8,128)} %bitcast.4, f32[256,128]{1,0:T(8,128)} %bitcast.5, s32[1,512]{1,0:T(1,128)} %cells_in.1, s32[1]{0:T(128)S(6)} %copy.8.counts_ref, f32[1,512]{1,0:T(1,128)} %innovations_in.1, f32[1,512]{1,0:T(1,128)} %precision_in.1), custom_call_target="tpu_custom_call" | custom-call | tf_op jit(solution)/shard_map/pallas_call | solution.py:710
  28.2 1.6 %broadcast_multiply_fusion = f32[256,128]{1,0:T(8,128)} fusion(f32[256,128]{1,0:T(8,128)} %shard_map.73), kind=kLoop, calls=%fused_computation | loop fusion | flops 32768 | bytes 262144 | tf_op jit(solution)/shard_map/mul | solution.py:755
